TPU v7x, 32 devices: a whole 2x2x4 slice. The times are simulated.
32 devices in a mesh: dp: 8 (over y, x, core), sp: 4 (over z).
Axes of the slice: x: 2, y: 2, z: 4, core: 2. Of those that a mesh axis runs over, the one named last changes fastest.
Arguments:
- inputs: bfloat16 [16, 2048, 768], P('dp', 'sp'), may hold values from -6 to 6
- out_grad: bfloat16 [16, 2048, 768], P('dp', 'sp'), may hold values from -6 to 6
- segment_ids: int32 [16, 2048], P('dp'), may hold values from 0 to 7, as said below
- positions: int32 [16, 2048], P('dp'), may hold values from 0 to 1023, as said below
- norm1_gain: bfloat16 [768], replicated, may hold values from 0.5 to 1.5
- norm1_bias: bfloat16 [768], replicated, may hold values from -1.75 to 1.75
- norm2_gain: bfloat16 [768], replicated, may hold values from 0.5 to 1.5
- norm2_bias: bfloat16 [768], replicated, may hold values from -1.75 to 1.75
- query_weight: bfloat16 [768, 768], replicated, may hold values from -0.21875 to 0.21875
- query_bias: bfloat16 [768], replicated, may hold values from -1.75 to 1.75
- key_weight: bfloat16 [768, 64], replicated, may hold values from -0.21875 to 0.21875
- key_bias: bfloat16 [16], replicated, may hold values from -1.75 to 1.75
- value_weight: bfloat16 [768, 64], replicated, may hold values from -0.21875 to 0.21875
- value_bias: bfloat16 [64], replicated, may hold values from -1.75 to 1.75
- output_weight: bfloat16 [768, 768], replicated, may hold values from -2.5 to 2.5
- output_bias: bfloat16 [768], replicated, may hold values from -1.75 to 1.75
- hidden_weight: bfloat16 [768, 3072], replicated, may hold values from -0.21875 to 0.21875
- hidden_bias: bfloat16 [3072], replicated, may hold values from -1.75 to 1.75
- down_weight: bfloat16 [3072, 768], replicated, may hold values from -0.109375 to 0.109375
- down_bias: bfloat16 [768], replicated, may hold values from -1.75 to 1.75
Outputs:
- layer_out: bfloat16 [16, 2048, 768], P('dp', 'sp')
- input_grad: float32 [16, 2048, 768], P('dp', 'sp')
- norm1_gain_grad: float32 [768], P('sp')
- norm1_bias_grad: float32 [768], P('sp')
- norm2_gain_grad: float32 [768], P('sp')
- norm2_bias_grad: float32 [768], P('sp')
- query_weight_grad: float32 [768, 768], P('sp')
- query_bias_grad: float32 [768], P('sp')
- key_weight_grad: float32 [768, 64], P('sp')
- key_bias_grad: float32 [16], P('sp')
- value_weight_grad: float32 [768, 64], P('sp')
- value_bias_grad: float32 [64], P('sp')
- output_weight_grad: float32 [768, 768], P('sp')
- output_bias_grad: float32 [768], P('sp')
- hidden_weight_grad: float32 [768, 3072], P('sp')
- hidden_bias_grad: float32 [3072], P('sp')
- down_weight_grad: float32 [3072, 768], P('sp')
- down_bias_grad: float32 [768], P('sp')
Inputs may be any that keep to these rules, and one draw needn't show every extreme that they name: `segment_ids`: document numbers of a row start at 0 and rise by one at each of its 7 boundaries, so every row holds exactly 8 documents; the first document of every row holds exactly 1024 tokens and each other document fewer. `positions`: each token's place counted from 0 at the first token of its document.
All inputs are finite; a program needn't handle non-finite values.
Results may differ from a plain program's by a relative error of at most 0.0085.
The roundings to bfloat16 on the way count: a program that leaves them out, or rounds other values in their place, can miss the bound.
Values may be sent and summed in bfloat16 or wider, within the bound.
No kernel may reach another device: no remote copies, remote signals or barrier semaphores. Data moves between devices by JAX's collectives and lax.ppermute only.
A program may use at most 256 MiB of HBM per device.

v0:
```python
import jax
import jax.numpy as jnp
from jax import lax
from jax.sharding import PartitionSpec as P

ROT = 16
EPSILON = 1e-05


def norm_forward(token_rows, gain_vec, offset):
    row_mean = jnp.mean(token_rows, -1, keepdims=True)
    centered = token_rows - row_mean
    inverse = lax.rsqrt(jnp.mean(centered * centered, -1, keepdims=True) + EPSILON)
    normed = centered * inverse
    return (normed * gain_vec + offset, normed, inverse)


def norm_backward(grad_out, normed, inverse, gain_vec):
    scaled = grad_out * gain_vec
    inner_sum = jnp.mean(scaled * normed, -1, keepdims=True)
    grad_in = inverse * (scaled - jnp.mean(scaled, -1, keepdims=True) - normed * inner_sum)
    return (grad_in, jnp.sum(grad_out * normed, 0), jnp.sum(grad_out, 0))


def rope_tables(places):
    half_rot = ROT // 2
    frequency = 10000.0 ** (-(jnp.arange(half_rot, dtype=jnp.float32) * 2.0) / ROT)
    angles = places.astype(jnp.float32)[:, None] * frequency[None, :]
    return (jnp.cos(angles), jnp.sin(angles))


def rotate(values_in, cosine, sine_tab):
    half_rot = ROT // 2
    first_part = values_in[..., :half_rot]
    second_part = values_in[..., half_rot:ROT]
    return jnp.concatenate(
        [
            first_part * cosine - second_part * sine_tab,
            second_part * cosine + first_part * sine_tab,
            values_in[..., ROT:],
        ],
        -1,
    )


def times_transposed(matrix_a, matrix_b):
    return lax.dot_general(
        matrix_a, matrix_b, (((1,), (1,)), ((), ())), preferred_element_type=jnp.float32
    )


def transposed_times(matrix_a, matrix_b):
    return lax.dot_general(
        matrix_a, matrix_b, (((0,), (0,)), ((), ())), preferred_element_type=jnp.float32
    )


def block_mask(seg_query, index_query, segments_all, block_start, block_end, key_end):
    key_index = jnp.arange(key_end, dtype=jnp.int32)
    same_doc = seg_query[block_start:block_end][:, None] == segments_all[None, :key_end]
    earlier = key_index[None, :] <= index_query[block_start:block_end][:, None]
    return (same_doc & earlier)[:, None, :]


def attend_forward(queries, keys_all, values_all, seg_query, index_query, segments_all):
    row_count = queries.shape[0]
    head_dim = keys_all.shape[1]
    heads_here = queries.shape[1] // head_dim
    full_len = keys_all.shape[0]
    block_rows = 512
    scale_factor = head_dim ** (-0.5)
    outputs, lse_list = ([], [])
    for block_start in range(0, row_count, block_rows):
        block_end = block_start + block_rows
        key_end = min(full_len, block_end)
        query_block = queries[block_start:block_end].reshape(block_rows, heads_here, head_dim)
        scores = (
            jnp.einsum(
                "qhd,kd->qhk", query_block, keys_all[:key_end], preferred_element_type=jnp.float32
            )
            * scale_factor
        )
        allowed = block_mask(seg_query, index_query, segments_all, block_start, block_end, key_end)
        masked = jnp.where(allowed, scores, -1e30)
        top_score = jnp.max(masked, -1, keepdims=True)
        exponent = jnp.exp(masked - top_score)
        total_weight = jnp.sum(exponent, -1, keepdims=True)
        weights_blk = (exponent / total_weight).astype(jnp.bfloat16)
        out_block = jnp.einsum(
            "qhk,kd->qhd", weights_blk, values_all[:key_end], preferred_element_type=jnp.float32
        )
        outputs.append(out_block.reshape(block_rows, heads_here * head_dim).astype(jnp.bfloat16))
        lse_list.append(top_score + jnp.log(total_weight))
    return (jnp.concatenate(outputs, 0), lse_list)


def attend_backward(
    queries, keys_all, values_all, grad_heads, lse_list, seg_query, index_query, segments_all
):
    row_count = queries.shape[0]
    head_dim = keys_all.shape[1]
    heads_here = queries.shape[1] // head_dim
    full_len = keys_all.shape[0]
    block_rows = 512
    scale_factor = head_dim ** (-0.5)
    grad_query_parts = []
    grad_kv = jnp.zeros((full_len, 2 * head_dim), jnp.float32)
    for block_number, block_start in enumerate(range(0, row_count, block_rows)):
        block_end = block_start + block_rows
        key_end = min(full_len, block_end)
        query_block = queries[block_start:block_end].reshape(block_rows, heads_here, head_dim)
        grad_block = grad_heads[block_start:block_end].reshape(block_rows, heads_here, head_dim)
        scores = (
            jnp.einsum(
                "qhd,kd->qhk", query_block, keys_all[:key_end], preferred_element_type=jnp.float32
            )
            * scale_factor
        )
        allowed = block_mask(seg_query, index_query, segments_all, block_start, block_end, key_end)
        masked = jnp.where(allowed, scores, -1e30)
        probs_f = jnp.exp(masked - lse_list[block_number])
        weights_blk = probs_f.astype(jnp.bfloat16)
        grad_weights = jnp.einsum(
            "qhd,kd->qhk", grad_block, values_all[:key_end], preferred_element_type=jnp.float32
        )
        row_inner = jnp.sum(probs_f * grad_weights, -1, keepdims=True)
        grad_scores = (probs_f * (grad_weights - row_inner)).astype(jnp.bfloat16)
        grad_query_block = (
            jnp.einsum(
                "qhk,kd->qhd", grad_scores, keys_all[:key_end], preferred_element_type=jnp.float32
            )
            * scale_factor
        )
        grad_key_part = (
            jnp.einsum("qhk,qhd->kd", grad_scores, query_block, preferred_element_type=jnp.float32)
            * scale_factor
        )
        grad_value_part = jnp.einsum(
            "qhk,qhd->kd", weights_blk, grad_block, preferred_element_type=jnp.float32
        )
        grad_kv = grad_kv.at[:key_end].add(jnp.concatenate([grad_key_part, grad_value_part], 1))
        grad_query_parts.append(grad_query_block.reshape(block_rows, heads_here * head_dim))
    return (jnp.concatenate(grad_query_parts, 0), grad_kv)


def gelu_exact(values_in):
    return jax.nn.gelu(values_in, approximate=False)


def one_row(
    token_in,
    grad_in_row,
    segments,
    places_full,
    norm1_gain,
    norm1_bias,
    norm2_gain,
    norm2_bias,
    query_weight,
    query_bias,
    key_weight,
    key_bias,
    value_weight,
    value_bias,
    output_weight,
    output_bias,
    hidden_weight,
    hidden_bias,
    down_weight,
    down_bias,
):
    sp_count = lax.axis_size("sp")
    local_len = token_in.shape[0]
    model_width = token_in.shape[1]
    head_dim = key_weight.shape[1]
    rot_dims = key_bias.shape[0]
    heads_all = model_width // head_dim
    full_len = local_len * sp_count
    start_row = lax.axis_index("sp") * local_len
    places_local = lax.dynamic_slice_in_dim(places_full, start_row, local_len)
    cos_local, sin_local = rope_tables(places_local)
    full_index = jnp.arange(full_len, dtype=jnp.int32)
    token_rows = token_in.astype(jnp.float32)
    norm_one, normed_one, inverse_one = norm_forward(
        token_rows, norm1_gain.astype(jnp.float32), norm1_bias.astype(jnp.float32)
    )
    attn_input = norm_one.astype(jnp.bfloat16)
    key_shift = jnp.concatenate(
        [key_bias.astype(jnp.float32), jnp.zeros((head_dim - rot_dims,), jnp.float32)]
    )
    query_pre = jnp.dot(
        attn_input, query_weight, preferred_element_type=jnp.float32
    ) + query_bias.astype(jnp.float32)
    key_pre = jnp.dot(attn_input, key_weight, preferred_element_type=jnp.float32) + key_shift
    value_pre = jnp.dot(
        attn_input, value_weight, preferred_element_type=jnp.float32
    ) + value_bias.astype(jnp.float32)
    query_rot = rotate(
        query_pre.reshape(local_len, heads_all, head_dim),
        cos_local[:, None, :],
        sin_local[:, None, :],
    )
    query_rot = query_rot.reshape(local_len, model_width).astype(jnp.bfloat16)
    key_rot = rotate(key_pre, cos_local, sin_local).astype(jnp.bfloat16)
    kv_local = jnp.concatenate([key_rot, value_pre.astype(jnp.bfloat16)], 1)
    kv_full = lax.all_gather(kv_local, "sp", axis=0, tiled=True)
    keys_all = kv_full[:, :head_dim]
    values_all = kv_full[:, head_dim:]
    queries = lax.all_to_all(query_rot, "sp", split_axis=1, concat_axis=0, tiled=True)
    heads_out, lse_list = attend_forward(
        queries, keys_all, values_all, segments, full_index, segments
    )
    attn_local = lax.all_to_all(heads_out, "sp", split_axis=0, concat_axis=1, tiled=True)
    attn_branch = jnp.dot(
        attn_local, output_weight, preferred_element_type=jnp.float32
    ) + output_bias.astype(jnp.float32)
    norm_two, normed_two, inverse_two = norm_forward(
        token_rows, norm2_gain.astype(jnp.float32), norm2_bias.astype(jnp.float32)
    )
    mlp_input = norm_two.astype(jnp.bfloat16)
    pre_act = jnp.dot(
        mlp_input, hidden_weight, preferred_element_type=jnp.float32
    ) + hidden_bias.astype(jnp.float32)
    activated, gelu_pull = jax.vjp(gelu_exact, pre_act)
    act_low = activated.astype(jnp.bfloat16)
    mlp_branch = jnp.dot(
        act_low, down_weight, preferred_element_type=jnp.float32
    ) + down_bias.astype(jnp.float32)
    layer_row = (token_rows + attn_branch + mlp_branch).astype(jnp.bfloat16)
    grad_rows_f = grad_in_row.astype(jnp.float32)
    grad_act = times_transposed(grad_in_row, down_weight)
    grad_pre_low = gelu_pull(grad_act)[0].astype(jnp.bfloat16)
    down_weight_grad = transposed_times(act_low, grad_in_row)
    down_bias_grad = jnp.sum(grad_rows_f, 0)
    hidden_weight_grad = transposed_times(mlp_input, grad_pre_low)
    hidden_bias_grad = jnp.sum(grad_pre_low.astype(jnp.float32), 0)
    grad_norm_two = times_transposed(grad_pre_low, hidden_weight)
    mlp_back, norm2_gain_grad, norm2_bias_grad = norm_backward(
        grad_norm_two, normed_two, inverse_two, norm2_gain.astype(jnp.float32)
    )
    grad_attn_low = times_transposed(grad_in_row, output_weight).astype(jnp.bfloat16)
    output_weight_grad = transposed_times(attn_local, grad_in_row)
    grad_heads = lax.all_to_all(grad_attn_low, "sp", split_axis=1, concat_axis=0, tiled=True)
    grad_queries, grad_kv = attend_backward(
        queries, keys_all, values_all, grad_heads, lse_list, segments, full_index, segments
    )
    cos_full, sin_full = rope_tables(places_full)
    heads_here = grad_queries.shape[1] // head_dim
    grad_query_full = rotate(
        grad_queries.reshape(full_len, heads_here, head_dim),
        cos_full[:, None, :],
        -sin_full[:, None, :],
    )
    grad_query_full = grad_query_full.reshape(full_len, heads_here * head_dim).astype(jnp.bfloat16)
    grad_query_local = lax.all_to_all(
        grad_query_full, "sp", split_axis=0, concat_axis=1, tiled=True
    )
    grad_kv_local = lax.psum_scatter(grad_kv, "sp", scatter_dimension=0, tiled=True)
    grad_key_low = rotate(grad_kv_local[:, :head_dim], cos_local, -sin_local).astype(jnp.bfloat16)
    grad_value_low = grad_kv_local[:, head_dim:].astype(jnp.bfloat16)
    query_weight_grad = transposed_times(attn_input, grad_query_local)
    query_bias_grad = jnp.sum(grad_query_local.astype(jnp.float32), 0)
    key_weight_grad = transposed_times(attn_input, grad_key_low)
    key_bias_grad = jnp.sum(grad_key_low[:, :rot_dims].astype(jnp.float32), 0)
    value_weight_grad = transposed_times(attn_input, grad_value_low)
    value_bias_grad = jnp.sum(grad_value_low.astype(jnp.float32), 0)
    grad_norm_one = (
        times_transposed(grad_query_local, query_weight)
        + times_transposed(grad_key_low, key_weight)
        + times_transposed(grad_value_low, value_weight)
    )
    attn_back, norm1_gain_grad, norm1_bias_grad = norm_backward(
        grad_norm_one, normed_one, inverse_one, norm1_gain.astype(jnp.float32)
    )
    input_row = grad_rows_f + attn_back + mlp_back
    grad_list = [
        norm1_gain_grad,
        norm1_bias_grad,
        norm2_gain_grad,
        norm2_bias_grad,
        query_weight_grad,
        query_bias_grad,
        key_weight_grad,
        key_bias_grad,
        value_weight_grad,
        value_bias_grad,
        output_weight_grad,
        down_bias_grad,
        hidden_weight_grad,
        hidden_bias_grad,
        down_weight_grad,
        down_bias_grad,
    ]
    return (layer_row, input_row, grad_list)


def on_device(
    inputs,
    out_grad,
    segment_ids,
    positions,
    norm1_gain,
    norm1_bias,
    norm2_gain,
    norm2_bias,
    query_weight,
    query_bias,
    key_weight,
    key_bias,
    value_weight,
    value_bias,
    output_weight,
    output_bias,
    hidden_weight,
    hidden_bias,
    down_weight,
    down_bias,
):
    sp_count = lax.axis_size("sp")
    params_all = (
        norm1_gain,
        norm1_bias,
        norm2_gain,
        norm2_bias,
        query_weight,
        query_bias,
        key_weight,
        key_bias,
        value_weight,
        value_bias,
        output_weight,
        output_bias,
        hidden_weight,
        hidden_bias,
        down_weight,
        down_bias,
    )
    layer_rows, input_rows = ([], [])
    grad_list = None
    for row_number in range(inputs.shape[0]):
        layer_row, input_row, row_grads = one_row(
            inputs[row_number],
            out_grad[row_number],
            segment_ids[row_number],
            positions[row_number],
            *params_all
        )
        layer_rows.append(layer_row)
        input_rows.append(input_row)
        if grad_list is None:
            grad_list = row_grads
        else:
            grad_list = [total + part for total, part in zip(grad_list, row_grads)]
    layer_out = jnp.stack(layer_rows, 0)
    input_grad = jnp.stack(input_rows, 0)
    flat_parts = [each_grad.reshape(sp_count, -1) for each_grad in grad_list]
    part_sizes = [piece.shape[1] for piece in flat_parts]
    packed = jnp.concatenate(flat_parts, 1)
    own_row = lax.psum_scatter(packed, "sp", scatter_dimension=0, tiled=True)
    summed = lax.psum(own_row, "dp").reshape(-1)
    results = []
    offset_now = 0
    for each_grad, size_now in zip(grad_list, part_sizes):
        shard_shape = (each_grad.shape[0] // sp_count,) + each_grad.shape[1:]
        results.append(summed[offset_now : offset_now + size_now].reshape(shard_shape))
        offset_now = offset_now + size_now
    return (layer_out, input_grad) + tuple(results)


def solution(mesh):
    placed = (
        P("dp", "sp", None),
        P("dp", "sp", None),
        P("dp", None),
        P("dp", None),
        P(),
        P(),
        P(),
        P(),
        P(),
        P(),
        P(),
        P(),
        P(),
        P(),
        P(),
        P(),
        P(),
        P(),
        P(),
        P(),
    )
    return jax.shard_map(
        on_device,
        mesh=mesh,
        in_specs=placed,
        out_specs=(
            P("dp", "sp", None),
            P("dp", "sp", None),
            P("sp"),
            P("sp"),
            P("sp"),
            P("sp"),
            P("sp", None),
            P("sp"),
            P("sp", None),
            P("sp"),
            P("sp", None),
            P("sp"),
            P("sp", None),
            P("sp"),
            P("sp", None),
            P("sp"),
            P("sp", None),
            P("sp"),
        ),
        check_vma=False,
    )
```

profile of v0, /device:TPU:0, one launch (start us, length us, event | category | flops | bytes accessed | tf_op | source)
XLA Modules:
  0.0 1696.9 jit_solution(9105256135938720582)
XLA Ops:
  10.8 6.3 all-to-all-start.4
  46.2 16.8 all_gather.7
  72.8 4.9 fusion.278
  77.7 34.7 %multiply_convert_fusion.7 = (bf16[512,3072]{1,0:T(8,128)(2,1)}, f32[512,3072]{1,0:T(8,128)}, bf16[512,3072]{1,0:T(8,128)(2,1)}, f32[512,3072]{1,0:T(8,128)}, f32[512,3072]{1,0:T(8,128)}) fusion(f32[3072]{0:T(1024)S(1)} %copy-done.121, f32[512,3072]{1,0:T(8,128)S(1)} %fusion.278, bf16[768,3072]{1,0:T(8,128)(2,1)S(1)} %bitcast.595, ...), kind=kOutput, calls=%fused_computation.66 | convolution fusion | flops 2625896448 | bytes 36986880 | tf_op jit(solution)/shard_map/dot_general | solution.py:221
  112.5 7.6 convert_reduce_fusion
  120.0 9.0 convert_reduce_fusion.1
  129.6 4.9 fusion.280
  134.6 5.6 convolution_add_fusion.1
  140.2 14.0 reshape.1321
  154.1 4.8 fusion.192
  158.9 5.4 convolution_add_fusion
  164.4 12.0 reshape.1322
  190.6 6.2 fusion.307
  196.8 5.5 all-to-all-start
  202.3 27.9 %all_gather.6 = bf16[2048,128]{0,1:T(8,128)(2,1)S(1)} all-gather(bf16[512,128]{0,1:T(8,128)(2,1)S(1)} %pad_maximum_fusion.10), channel_id=1, replica_groups=mesh['dp'=8,'sp'=4] {'sp'}, dimensions={0}, use_global_device_ids=true | all-gather | bytes 655360 | tf_op jit(solution)/shard_map/all_gather | solution.py:206
  230.2 7.1 fusion.305
  252.7 7.2 all-to-all-done.2
  259.9 4.6 all-to-all-start.6
  271.1 9.9 all-to-all-done.6
  328.4 4.6 multiply_reduce_fusion.3
  333.0 5.2 multiply_convert_fusion.3
  357.8 6.0 fusion.298
  363.8 6.4 fusion
  370.3 7.8 fusion.157
  381.5 8.6 multiply_reduce_fusion.1
  390.1 9.4 multiply_convert_fusion.1
  404.3 5.9 multiply_reduce_fusion
  410.2 6.5 multiply_convert_fusion
  438.3 8.3 all-to-all-done.3
  446.6 4.2 all-to-all-start.1
  464.2 6.2 fusion.59
  470.6 6.7 all-to-all-done.1
  490.3 7.5 fusion.67
  512.5 4.2 reshape.1320
  520.3 16.7 all-to-all-done.7
  537.0 4.4 convolution_add_fusion.3
  541.4 4.3 reshape.1317
  584.0 5.2 fusion.110
  610.2 13.7 dynamic-update-slice.32
  625.4 49.6 %dynamic-update-slice.34 = f32[4,1501268]{1,0:T(4,128)} dynamic-update-slice(f32[4,1501268]{1,0:T(4,128)} %dynamic-update-slice.33, f32[4,589824]{1,0:T(4,128)} %reshape.1321, s32[]{} %constant.345, s32[]{} %constant.357) | dynamic-update-slice | bytes 18874372
  676.5 49.2 %dynamic-update-slice.36 = f32[4,1501268]{1,0:T(4,128)} dynamic-update-slice(f32[4,1501268]{1,0:T(4,128)} %dynamic-update-slice.35, f32[4,589824]{1,0:T(4,128)} %reshape.1322, s32[]{} %constant.345, s32[]{} %constant.359) | dynamic-update-slice | bytes 18874372
  728.4 7.1 fusion.302
  735.5 788.8 %all-reduce.9.cloned.1.call-done = f32[4,1501268]{1,0:T(4,128)} async-done(((f32[4,1501268]{1,0:T(4,128)}), f32[4,1501268]{1,0:T(4,128)}) %all-reduce.9.cloned.1.call-update) | async-done | bytes 24020304
  1524.2 12.7 constant_dynamic-slice_fusion
  1536.9 6.0 fusion.303
  1551.1 86.1 %all-reduce.7.cloned.1.call-done = f32[1,1501268]{1,0:T(1,128)} async-done(((f32[1,1501268]{1,0:T(1,128)}), f32[1,1501268]{1,0:T(1,128)}) %all-reduce.7.cloned.1.call-update) | async-done | bytes 6005088 | tf_op jit(solution)/shard_map/psum | solution.py:360
  1640.0 27.6 %slice_reduce_fusion = (f32[589824]{0:T(1024)}, f32[589824]{0:T(1024)S(1)}) fusion(f32[1,1501268]{1,0:T(1,128)} %all-reduce.7.cloned.1.call-done), kind=kLoop, calls=%fused_computation.133 | loop fusion | bytes 9437184 | tf_op jit(solution)/shard_map/slice | solution.py:365
  1670.9 8.6 slice_reduce_fusion.2
  (550 shorter events, 309.3 us)
Async XLA Ops:
  7.2 26.2 %copy-start = (bf16[768,768]{1,0:T(8,128)(2,1)S(1)}, bf16[768,768]{1,0:T(8,128)(2,1)}, u32[]{:S(2)}) copy-start(bf16[768,768]{1,0:T(8,128)(2,1)} %param.48) | copy-start | bytes 3538948
  7.2 12.8 copy-start.89
  9.6 17.9 %copy-start.9 = (bf16[2,512,768]{2,1,0:T(8,128)(2,1)S(1)}, bf16[2,512,768]{2,1,0:T(8,128)(2,1)}, u32[]{:S(2)}) copy-start(bf16[2,512,768]{2,1,0:T(8,128)(2,1)} %param.40) | copy-start | bytes 4718596
  10.8 186.0 %all-to-all-start.4 = ((bf16[512,4,192]{0,2,1:T(8,128)(2,1)}), bf16[512,4,192]{0,2,1:T(8,128)(2,1)}, u32[]{:S(2)}, u32[]{:S(2)}) async-start(bf16[512,4,192]{0,2,1:T(8,128)(2,1)} %bitcast.61), calls=%async_computation.4 | async-start | bytes 1572864 | tf_op jit(solution)/shard_map/all_to_all | solution.py:243
  27.9 101.8 %copy-start.85 = (f32[512]{0:T(512)}, f32[512]{0:T(512)S(1)}, u32[]{:S(2)}) copy-start(f32[512]{0:T(512)S(1)} %get-tuple-element.347) | copy-start | bytes 6148
  28.5 101.1 %copy-start.90 = (f32[512]{0:T(512)}, f32[512]{0:T(512)S(1)}, u32[]{:S(2)}) copy-start(f32[512]{0:T(512)S(1)} %add_rsqrt_fusion.1) | copy-start | bytes 6148
  37.3 97.3 %copy-start.71 = (f32[768]{0:T(1024)}, f32[768]{0:T(1024)S(1)}, u32[]{:S(2)}) copy-start(f32[768]{0:T(1024)S(1)} %convert_element_type.350) | copy-start | bytes 9220
  44.3 26.9 %copy-start.115 = (f32[1,512]{1,0:T(1,128)}, f32[1,512]{1,0:T(1,128)S(1)}, u32[]{:S(2)}) copy-start(f32[1,512]{1,0:T(1,128)S(1)} %get-tuple-element.348) | copy-start | bytes 6148
  44.3 26.9 %copy-start.117 = (f32[1,512]{1,0:T(1,128)}, f32[1,512]{1,0:T(1,128)S(1)}, u32[]{:S(2)}) copy-start(f32[1,512]{1,0:T(1,128)S(1)} %get-tuple-element.349) | copy-start | bytes 6148
  72.8 39.6 %slice-start.5 = ((s8[4718592]{0:T(1024)(128)(4,1)}), s8[4194304]{0:T(1024)(128)(4,1)S(1)}, s32[]{:S(2)}) async-start(s8[4718592]{0:T(1024)(128)(4,1)} %bitcast.596), calls=%async_computation.19 | async-start | bytes 8388608
  77.7 34.7 %copy-start.14 = (bf16[2,512,768]{2,1,0:T(8,128)(2,1)S(1)}, bf16[2,512,768]{2,1,0:T(8,128)(2,1)}, u32[]{:S(2)}) copy-start(bf16[2,512,768]{2,1,0:T(8,128)(2,1)} %param.41) | copy-start | bytes 4718596
  77.7 34.7 %slice-start.6 = ((s8[4718592]{0:T(1024)(128)(4,1)}), s8[524288]{0:T(1024)(128)(4,1)S(1)}, s32[]{:S(2)}) async-start(s8[4718592]{0:T(1024)(128)(4,1)} %bitcast.596), calls=%async_computation.20 | async-start | bytes 1048576
  140.2 14.0 copy-start.15
  164.4 14.4 copy-start.113
  164.4 14.4 copy-start.114
  164.4 14.4 copy-start.131
  164.4 15.7 copy-start.35
  180.1 10.5 copy-start.34
  196.8 42.6 %all-to-all-start = ((bf16[512,4,192]{0,2,1:T(8,128)(2,1)}), bf16[512,4,192]{0,2,1:T(8,128)(2,1)S(1)}, u32[]{:S(2)}, u32[]{:S(2)}) async-start(bf16[512,4,192]{0,2,1:T(8,128)(2,1)} %bitcast.4), calls=%async_computation | async-start | bytes 1572864 | tf_op jit(solution)/shard_map/all_to_all | solution.py:209
  240.3 19.7 %all-to-all-start.2 = ((bf16[512,4,192]{0,2,1:T(8,128)(2,1)}), bf16[512,4,192]{0,2,1:T(8,128)(2,1)S(1)}, u32[]{:S(2)}, u32[]{:S(2)}) async-start(bf16[512,4,192]{0,2,1:T(8,128)(2,1)} %bitcast.34), calls=%async_computation.2 | async-start | bytes 1572864 | tf_op jit(solution)/shard_map/all_to_all | solution.py:209
  250.3 15.8 copy-start.22
  250.3 15.8 copy-start.78
  259.9 21.1 %all-to-all-start.6 = ((bf16[512,4,192]{0,2,1:T(8,128)(2,1)}), bf16[512,4,192]{0,2,1:T(8,128)(2,1)}, u32[]{:S(2)}, u32[]{:S(2)}) async-start(bf16[512,4,192]{0,2,1:T(8,128)(2,1)} %bitcast.80), calls=%async_computation.7 | async-start | bytes 1572864 | tf_op jit(solution)/shard_map/all_to_all | solution.py:243
  267.2 18.8 %copy-start.94 = (f32[512,3]{0,1:T(4,128)}, f32[512,3]{0,1:T(4,128)S(1)}, u32[]{:S(2)}) copy-start(f32[512,3]{0,1:T(4,128)S(1)} %log_add_fusion.3) | copy-start | bytes 18436
  283.2 24.8 %copy-start.40 = (bf16[1,512,192]{1,2,0:T(8,128)(2,1)}, bf16[1,512,192]{1,2,0:T(8,128)(2,1)S(1)}, u32[]{:S(2)}) copy-start(bf16[1,512,192]{1,2,0:T(8,128)(2,1)S(1)} %get-tuple-element.249) | copy-start | bytes 589828
  290.7 18.8 %copy-start.3 = (f32[512,3,1024]{2,0,1:T(8,128)}, f32[512,3,1024]{2,0,1:T(8,128)S(1)}, u32[]{:S(2)}) copy-start(f32[512,3,1024]{2,0,1:T(8,128)S(1)} %get-tuple-element.314) | copy-start | bytes 18874372
  292.3 17.3 %copy-start.92 = (f32[512,3]{0,1:T(4,128)}, f32[512,3]{0,1:T(4,128)S(1)}, u32[]{:S(2)}) copy-start(f32[512,3]{0,1:T(4,128)S(1)} %log_add_fusion.2) | copy-start | bytes 18436
  316.2 27.9 %copy-start.2 = (f32[512,3,1536]{2,0,1:T(8,128)}, f32[512,3,1536]{2,0,1:T(8,128)S(1)}, u32[]{:S(2)}) copy-start(f32[512,3,1536]{2,0,1:T(8,128)S(1)} %get-tuple-element.312) | copy-start | bytes 28311556
  353.1 57.2 %copy-start.1 = (f32[512,3,2048]{2,0,1:T(8,128)}, f32[512,3,2048]{2,0,1:T(8,128)S(1)}, u32[]{:S(2)}) copy-start(f32[512,3,2048]{2,0,1:T(8,128)S(1)} %get-tuple-element.310) | copy-start | bytes 37748740
  422.5 24.0 %all-to-all-start.3 = ((bf16[4,512,192]{1,2,0:T(8,128)(2,1)}), bf16[4,512,192]{1,2,0:T(8,128)(2,1)S(1)}, u32[]{:S(2)}, u32[]{:S(2)}) async-start(bf16[4,512,192]{1,2,0:T(8,128)(2,1)} %bitcast.510), calls=%async_computation.3 | async-start | bytes 1572864 | tf_op jit(solution)/shard_map/all_to_all | solution.py:213
  426.2 128.1 %reduce-scatter.3.cloned.1.call-start = ((), (), s32[]{:S(2)}) async-start(), calls=%async_computation.10 | async-start | bytes 1310720 | tf_op jit(solution)/shard_map/reduce_scatter | solution.py:258
  437.5 22.6 %copy-start.93 = (f32[512,3]{0,1:T(4,128)S(1)}, f32[512,3]{0,1:T(4,128)}, u32[]{:S(2)}) copy-start(f32[512,3]{0,1:T(4,128)} %copy-done.92) | copy-start | bytes 18436
  446.6 17.7 %copy-start.28 = (bf16[4,512,192]{1,2,0:T(8,128)(2,1)}, bf16[4,512,192]{1,2,0:T(8,128)(2,1)S(1)}, u32[]{:S(2)}) copy-start(bf16[4,512,192]{1,2,0:T(8,128)(2,1)S(1)} %all-to-all-done.3) | copy-start | bytes 2359300
  446.6 30.7 %all-to-all-start.1 = ((bf16[4,512,192]{1,2,0:T(8,128)(2,1)}), bf16[4,512,192]{1,2,0:T(8,128)(2,1)}, u32[]{:S(2)}, u32[]{:S(2)}) async-start(bf16[4,512,192]{1,2,0:T(8,128)(2,1)} %bitcast.526), calls=%async_computation.1 | async-start | bytes 1572864 | tf_op jit(solution)/shard_map/all_to_all | solution.py:213
  477.3 23.3 %all-to-all-start.5 = ((bf16[4,512,192]{1,2,0:T(8,128)(2,1)}), bf16[4,512,192]{1,2,0:T(8,128)(2,1)S(1)}, u32[]{:S(2)}, u32[]{:S(2)}) async-start(bf16[4,512,192]{1,2,0:T(8,128)(2,1)} %copy.106), calls=%async_computation.5 | async-start | bytes 1572864 | tf_op jit(solution)/shard_map/all_to_all | solution.py:255
  497.7 10.4 copy-start.16
  501.5 35.5 %all-to-all-start.7 = ((bf16[4,512,192]{1,2,0:T(8,128)(2,1)}), bf16[4,512,192]{1,2,0:T(8,128)(2,1)S(1)}, u32[]{:S(2)}, u32[]{:S(2)}) async-start(bf16[4,512,192]{1,2,0:T(8,128)(2,1)} %copy.111), calls=%async_computation.8 | async-start | bytes 1572864 | tf_op jit(solution)/shard_map/all_to_all | solution.py:255
  505.0 53.6 %reduce-scatter.5.cloned.1.call-start = ((), (), s32[]{:S(2)}) async-start(), calls=%async_computation.11 | async-start | bytes 1310720 | tf_op jit(solution)/shard_map/reduce_scatter | solution.py:258
  507.7 1016.6 %all-reduce.9.cloned.1.call-start = ((), (), s32[]{:S(2)}) async-start(), calls=%async_computation.13 | async-start | bytes 48041984
  512.5 24.5 %copy-start.100 = (f32[512]{0:T(512)S(1)}, f32[512]{0:T(512)}, u32[]{:S(2)}) copy-start(f32[512]{0:T(512)} %copy-done.98) | copy-start | bytes 6148
  537.0 10.1 copy-start.20
  547.9 12.4 copy-start.116
  551.0 15.5 copy-start.12
  593.1 10.0 copy-start.68
  593.1 12.1 copy-start.133
  593.1 15.7 copy-start.132
  625.4 49.6 %copy-start.105 = (f32[4,768]{1,0:T(4,128)S(1)}, f32[4,768]{1,0:T(4,128)}, u32[]{:S(2)}) copy-start(f32[4,768]{1,0:T(4,128)} %add.500) | copy-start | bytes 36868
  727.2 910.0 %all-reduce.7.cloned.1.call-start = ((), (), s32[]{:S(2)}) async-start(), calls=%async_computation.12 | async-start | bytes 12010496 | tf_op jit(solution)/shard_map/psum | solution.py:360
  (114 other events, 558.5 us)
Sparse Core Ops, SparseCore 0:
  432.3 37.6 reduce-scatter.2
  508.2 33.9 reduce-scatter.4
  727.3 796.9 all-reduce.8
  1537.0 100.1 all-reduce.6
where the time goes:
time: 1710 us; the launch traced here: 1700 us
  waiting for transfers between devices  927 us (54%)
  local copies, waits for them, and re-layouts  289 us (17%)
  matrix products  281 us (16%)
  other arithmetic  104 us (6%)
  blocking collectives  44.7 us (3%)
  starting transfers between devices  35.8 us (2%)
    unnamed x5, waiting for transfers between devices  789 us
    unnamed x319, local copies, waits for them, and re-layouts  155 us
    psum x1, waiting for transfers between devices, on_device(): summed = lax.psum(own_row, 'dp').reshape(-1)  86.1 us
    dot_general x12, matrix products, times_transposed(): lax.dot_general(matrix_a, matrix_b, (((1,), (1,)), ((), ())), preferred_e...  53.4 us
    all_gather x2, blocking collectives, one_row(): kv_full = lax.all_gather(kv_local, 'sp', axis=0, tiled=True)  44.7 us
    slice x7, local copies, waits for them, and re-layouts, on_device(): summed[offset_now:offset_now + size_now].reshape(shard_shape)  42.4 us
    dot_general x12, matrix products, transposed_times(): lax.dot_general(matrix_a, matrix_b, (((0,), (0,)), ((), ())), preferred_e...  41 us
    dot_general x2, matrix products, one_row(): jnp.dot(mlp_input, hidden_weight, preferred_element_type=jnp.float32)  39.5 us
  transfers between devices with their start and end apart: 12, of which 8 were waited for; matrix products, arithmetic and copies ran while one was open for 17% of the time, Pallas kernels for 0%

commit v1 on v0

--- a/solution.py
+++ b/solution.py
@@ -357,7 +357,7 @@
     part_sizes = [piece.shape[1] for piece in flat_parts]
     packed = jnp.concatenate(flat_parts, 1)
     own_row = lax.psum_scatter(packed, "sp", scatter_dimension=0, tiled=True)
-    summed = lax.psum(own_row, "dp").reshape(-1)
+    summed = jnp.sum(lax.all_gather(own_row, "dp"), axis=0).reshape(-1)
     results = []
     offset_now = 0
     for each_grad, size_now in zip(grad_list, part_sizes):

time: 1710 us -> 2060 us (1.20)
  other arithmetic: 104 us -> 308 us
  waiting for transfers between devices: 927 us -> 1050 us
  local copies, waits for them, and re-layouts: 289 us -> 313 us
    reduce_sum x0 -> x1, other arithmetic: none -> 204 us  [on_device(): summed = jnp.sum(lax.all_gather(own_row, 'dp'), axis=0).reshape(-1)]
    all_gather x0 -> x1, waiting for transfers between devices: none -> 199 us  [on_device(): summed = jnp.sum(lax.all_gather(own_row, 'dp'), axis=0).reshape(-1)]
    psum x1 -> x0, waiting for transfers between devices: 86.1 us -> none  [on_device(): summed = lax.psum(own_row, 'dp').reshape(-1)]
    reduce_sum x0 -> x1, local copies, waits for them, and re-layouts: none -> 23.4 us  [on_device(): summed = jnp.sum(lax.all_gather(own_row, 'dp'), axis=0).reshape(-1)]
  transfers between devices with their start and end apart: 12 -> 12, of which waited for: 8 -> 8; matrix products, arithmetic and copies ran while one was open for 17% -> 14% of each run, Pallas kernels for 0% -> 0%
where the time goes in v1:
time: 2060 us; the launch traced here: 2050 us
  waiting for transfers between devices  1050 us (51%)
  local copies, waits for them, and re-layouts  313 us (15%)
  other arithmetic  308 us (15%)
  matrix products  281 us (14%)
  blocking collectives  44.7 us (2%)
  starting transfers between devices  35.8 us (2%)
    unnamed x5, waiting for transfers between devices  796 us
    reduce_sum x1, other arithmetic, on_device(): summed = jnp.sum(lax.all_gather(own_row, 'dp'), axis=0).reshape(-1)  204 us
    all_gather x1, waiting for transfers between devices, on_device(): summed = jnp.sum(lax.all_gather(own_row, 'dp'), axis=0).reshape(-1)  199 us
    unnamed x319, local copies, waits for them, and re-layouts  158 us
    dot_general x12, matrix products, times_transposed(): lax.dot_general(matrix_a, matrix_b, (((1,), (1,)), ((), ())), preferred_e...  53.4 us
    all_gather x2, blocking collectives, one_row(): kv_full = lax.all_gather(kv_local, 'sp', axis=0, tiled=True)  44.7 us
  transfers between devices with their start and end apart: 12, of which 8 were waited for; matrix products, arithmetic and copies ran while one was open for 14% of the time, Pallas kernels for 0%

profile of v1, /device:TPU:0, one launch (start us, length us, event | category | flops | bytes accessed | tf_op | source)
XLA Modules:
  0.0 2045.1 jit_solution(5327707878377301415)
XLA Ops:
  10.8 6.3 all-to-all-start.4
  46.2 16.8 all_gather.13
  72.8 4.8 fusion.278
  77.7 34.7 %multiply_convert_fusion.7 = (bf16[512,3072]{1,0:T(8,128)(2,1)}, f32[512,3072]{1,0:T(8,128)}, bf16[512,3072]{1,0:T(8,128)(2,1)}, f32[512,3072]{1,0:T(8,128)}, f32[512,3072]{1,0:T(8,128)}) fusion(f32[3072]{0:T(1024)S(1)} %copy-done.122, f32[512,3072]{1,0:T(8,128)S(1)} %fusion.278, bf16[768,3072]{1,0:T(8,128)(2,1)S(1)} %bitcast.597, ...), kind=kOutput, calls=%fused_computation.66 | convolution fusion | flops 2625896448 | bytes 36986880 | tf_op jit(solution)/shard_map/dot_general | solution.py:221
  112.5 7.6 convert_reduce_fusion
  120.0 9.0 convert_reduce_fusion.1
  129.6 4.9 fusion.280
  134.6 5.6 convolution_add_fusion.1
  140.2 14.0 reshape.1322
  154.1 4.8 fusion.192
  158.9 5.4 convolution_add_fusion
  164.4 12.0 reshape.1323
  190.6 6.2 fusion.307
  196.8 5.5 all-to-all-start
  202.3 27.9 %all_gather.12 = bf16[2048,128]{0,1:T(8,128)(2,1)S(1)} all-gather(bf16[512,128]{0,1:T(8,128)(2,1)S(1)} %pad_maximum_fusion.10), channel_id=1, replica_groups=mesh['dp'=8,'sp'=4] {'sp'}, dimensions={0}, use_global_device_ids=true | all-gather | bytes 655360 | tf_op jit(solution)/shard_map/all_gather | solution.py:206
  230.2 7.1 fusion.305
  252.7 7.2 all-to-all-done.2
  259.9 4.6 all-to-all-start.6
  271.1 9.9 all-to-all-done.6
  328.4 4.6 multiply_reduce_fusion.3
  333.0 5.2 multiply_convert_fusion.3
  357.8 6.0 fusion.298
  363.8 6.4 fusion
  370.3 7.8 fusion.157
  381.5 8.6 multiply_reduce_fusion.1
  390.1 9.4 multiply_convert_fusion.1
  404.3 5.9 multiply_reduce_fusion
  410.2 6.5 multiply_convert_fusion
  438.3 8.6 all-to-all-done.3
  464.6 6.2 fusion.59
  470.9 6.4 all-to-all-done.1
  490.3 7.5 fusion.67
  520.4 16.6 all-to-all-done.7
  537.0 4.4 convolution_add_fusion.3
  541.4 4.3 reshape.1318
  584.0 5.2 fusion.110
  610.2 13.7 dynamic-update-slice.32
  625.4 49.6 %dynamic-update-slice.34 = f32[4,1501268]{1,0:T(4,128)} dynamic-update-slice(f32[4,1501268]{1,0:T(4,128)} %dynamic-update-slice.33, f32[4,589824]{1,0:T(4,128)} %reshape.1322, s32[]{} %constant.345, s32[]{} %constant.357) | dynamic-update-slice | bytes 18874372
  676.5 49.2 %dynamic-update-slice.36 = f32[4,1501268]{1,0:T(4,128)} dynamic-update-slice(f32[4,1501268]{1,0:T(4,128)} %dynamic-update-slice.35, f32[4,589824]{1,0:T(4,128)} %reshape.1323, s32[]{} %constant.345, s32[]{} %constant.359) | dynamic-update-slice | bytes 18874372
  728.3 795.9 %all-reduce.6.cloned.1.call-done = f32[4,1501268]{1,0:T(4,128)} async-done(((f32[4,1501268]{1,0:T(4,128)}), f32[4,1501268]{1,0:T(4,128)}) %all-reduce.6.cloned.1.call-update) | async-done | bytes 24020304
  1524.2 12.4 dynamic-slice_bitcast_fusion
  1537.3 6.0 fusion.302
  1543.4 6.6 fusion.303
  1559.0 199.5 %all-gather.4.cloned.1.call-done = f32[8,1,1501268]{2,1,0:T(1,128)} async-done(((f32[1,1,1501268]{2,1,0:T(1,128)}), f32[8,1,1501268]{2,1,0:T(1,128)}) %all-gather.4.cloned.1.call-update) | async-done | bytes 48040592 | tf_op jit(solution)/shard_map/all_gather | solution.py:360
  1758.4 204.3 %reduce.23 = f32[1501268]{0:T(1024)} reduce(f32[8,1,1501268]{2,1,0:T(1,128)} %all-gather.4.cloned.1.call-done, f32[]{:T(128)} %constant.273.clone.1), dimensions={0,1}, to_apply=%region_57.58 | reduce | flops 10508876 | bytes 54045652 | tf_op jit(solution)/shard_map/reduce_sum | solution.py:360
  1962.7 23.4 %reduce_sum.488 = f32[1,1501268]{1,0:T(1,128)S(1)} reshape(f32[1501268]{0:T(1024)} %reduce.23) | data formatting | bytes 12010144 | tf_op jit(solution)/shard_map/reduce_sum | solution.py:360
  1989.6 7.3 slice_reduce_fusion.2
  1996.8 26.4 %slice_reduce_fusion = (f32[589824]{0:T(1024)}, f32[589824]{0:T(1024)S(1)}) fusion(f32[1,1501268]{1,0:T(1,128)S(1)} %reduce_sum.488), kind=kLoop, calls=%fused_computation.134 | loop fusion | bytes 9437184 | tf_op jit(solution)/shard_map/slice | solution.py:365
  (552 shorter events, 321.0 us)
Async XLA Ops:
  7.2 26.2 %copy-start = (bf16[768,768]{1,0:T(8,128)(2,1)S(1)}, bf16[768,768]{1,0:T(8,128)(2,1)}, u32[]{:S(2)}) copy-start(bf16[768,768]{1,0:T(8,128)(2,1)} %param.48) | copy-start | bytes 3538948
  7.2 12.8 copy-start.90
  9.6 17.9 copy-start.9
  10.8 186.0 %all-to-all-start.4 = ((bf16[512,4,192]{0,2,1:T(8,128)(2,1)}), bf16[512,4,192]{0,2,1:T(8,128)(2,1)}, u32[]{:S(2)}, u32[]{:S(2)}) async-start(bf16[512,4,192]{0,2,1:T(8,128)(2,1)} %bitcast.61), calls=%async_computation.4 | async-start | bytes 1572864 | tf_op jit(solution)/shard_map/all_to_all | solution.py:243
  27.9 101.8 %copy-start.86 = (f32[512]{0:T(512)}, f32[512]{0:T(512)S(1)}, u32[]{:S(2)}) copy-start(f32[512]{0:T(512)S(1)} %get-tuple-element.347) | copy-start | bytes 6148
  28.5 101.1 %copy-start.91 = (f32[512]{0:T(512)}, f32[512]{0:T(512)S(1)}, u32[]{:S(2)}) copy-start(f32[512]{0:T(512)S(1)} %add_rsqrt_fusion.1) | copy-start | bytes 6148
  37.3 97.3 %copy-start.72 = (f32[768]{0:T(1024)}, f32[768]{0:T(1024)S(1)}, u32[]{:S(2)}) copy-start(f32[768]{0:T(1024)S(1)} %convert_element_type.350) | copy-start | bytes 9220
  44.3 26.9 %copy-start.116 = (f32[1,512]{1,0:T(1,128)}, f32[1,512]{1,0:T(1,128)S(1)}, u32[]{:S(2)}) copy-start(f32[1,512]{1,0:T(1,128)S(1)} %get-tuple-element.348) | copy-start | bytes 6148
  44.3 26.9 %copy-start.118 = (f32[1,512]{1,0:T(1,128)}, f32[1,512]{1,0:T(1,128)S(1)}, u32[]{:S(2)}) copy-start(f32[1,512]{1,0:T(1,128)S(1)} %get-tuple-element.349) | copy-start | bytes 6148
  72.8 39.6 %slice-start.5 = ((s8[4718592]{0:T(1024)(128)(4,1)}), s8[4194304]{0:T(1024)(128)(4,1)S(1)}, s32[]{:S(2)}) async-start(s8[4718592]{0:T(1024)(128)(4,1)} %bitcast.598), calls=%async_computation.19 | async-start | bytes 8388608
  77.7 34.7 %copy-start.14 = (bf16[2,512,768]{2,1,0:T(8,128)(2,1)S(1)}, bf16[2,512,768]{2,1,0:T(8,128)(2,1)}, u32[]{:S(2)}) copy-start(bf16[2,512,768]{2,1,0:T(8,128)(2,1)} %param.41) | copy-start | bytes 4718596
  77.7 34.7 %slice-start.6 = ((s8[4718592]{0:T(1024)(128)(4,1)}), s8[524288]{0:T(1024)(128)(4,1)S(1)}, s32[]{:S(2)}) async-start(s8[4718592]{0:T(1024)(128)(4,1)} %bitcast.598), calls=%async_computation.20 | async-start | bytes 1048576
  140.2 14.0 copy-start.15
  164.4 14.4 copy-start.114
  164.4 14.4 copy-start.115
  164.4 14.4 copy-start.132
  164.4 15.7 copy-start.36
  180.1 10.5 copy-start.35
  196.8 42.6 %all-to-all-start = ((bf16[512,4,192]{0,2,1:T(8,128)(2,1)}), bf16[512,4,192]{0,2,1:T(8,128)(2,1)S(1)}, u32[]{:S(2)}, u32[]{:S(2)}) async-start(bf16[512,4,192]{0,2,1:T(8,128)(2,1)} %bitcast.4), calls=%async_computation | async-start | bytes 1572864 | tf_op jit(solution)/shard_map/all_to_all | solution.py:209
  240.3 19.7 all-to-all-start.2
  250.3 15.8 copy-start.23
  250.3 15.8 copy-start.79
  259.9 21.1 %all-to-all-start.6 = ((bf16[512,4,192]{0,2,1:T(8,128)(2,1)}), bf16[512,4,192]{0,2,1:T(8,128)(2,1)}, u32[]{:S(2)}, u32[]{:S(2)}) async-start(bf16[512,4,192]{0,2,1:T(8,128)(2,1)} %bitcast.80), calls=%async_computation.7 | async-start | bytes 1572864 | tf_op jit(solution)/shard_map/all_to_all | solution.py:243
  267.2 18.8 copy-start.95
  283.2 24.8 %copy-start.41 = (bf16[1,512,192]{1,2,0:T(8,128)(2,1)}, bf16[1,512,192]{1,2,0:T(8,128)(2,1)S(1)}, u32[]{:S(2)}) copy-start(bf16[1,512,192]{1,2,0:T(8,128)(2,1)S(1)} %get-tuple-element.249) | copy-start | bytes 589828
  290.7 18.8 copy-start.3
  292.3 17.3 copy-start.93
  316.2 27.9 %copy-start.2 = (f32[512,3,1536]{2,0,1:T(8,128)}, f32[512,3,1536]{2,0,1:T(8,128)S(1)}, u32[]{:S(2)}) copy-start(f32[512,3,1536]{2,0,1:T(8,128)S(1)} %get-tuple-element.312) | copy-start | bytes 28311556
  353.1 57.2 %copy-start.1 = (f32[512,3,2048]{2,0,1:T(8,128)}, f32[512,3,2048]{2,0,1:T(8,128)S(1)}, u32[]{:S(2)}) copy-start(f32[512,3,2048]{2,0,1:T(8,128)S(1)} %get-tuple-element.310) | copy-start | bytes 37748740
  422.5 24.4 %all-to-all-start.3 = ((bf16[4,512,192]{1,2,0:T(8,128)(2,1)}), bf16[4,512,192]{1,2,0:T(8,128)(2,1)S(1)}, u32[]{:S(2)}, u32[]{:S(2)}) async-start(bf16[4,512,192]{1,2,0:T(8,128)(2,1)} %bitcast.512), calls=%async_computation.3 | async-start | bytes 1572864 | tf_op jit(solution)/shard_map/all_to_all | solution.py:213
  426.2 128.0 %reduce-scatter.3.cloned.1.call-start = ((), (), s32[]{:S(2)}) async-start(), calls=%async_computation.10 | async-start | bytes 1310720 | tf_op jit(solution)/shard_map/reduce_scatter | solution.py:258
  437.5 22.9 %copy-start.94 = (f32[512,3]{0,1:T(4,128)S(1)}, f32[512,3]{0,1:T(4,128)}, u32[]{:S(2)}) copy-start(f32[512,3]{0,1:T(4,128)} %copy-done.93) | copy-start | bytes 18436
  446.9 17.6 copy-start.29
  446.9 30.4 %all-to-all-start.1 = ((bf16[4,512,192]{1,2,0:T(8,128)(2,1)}), bf16[4,512,192]{1,2,0:T(8,128)(2,1)}, u32[]{:S(2)}, u32[]{:S(2)}) async-start(bf16[4,512,192]{1,2,0:T(8,128)(2,1)} %bitcast.528), calls=%async_computation.1 | async-start | bytes 1572864 | tf_op jit(solution)/shard_map/all_to_all | solution.py:213
  477.3 23.3 %all-to-all-start.5 = ((bf16[4,512,192]{1,2,0:T(8,128)(2,1)}), bf16[4,512,192]{1,2,0:T(8,128)(2,1)S(1)}, u32[]{:S(2)}, u32[]{:S(2)}) async-start(bf16[4,512,192]{1,2,0:T(8,128)(2,1)} %copy.106), calls=%async_computation.5 | async-start | bytes 1572864 | tf_op jit(solution)/shard_map/all_to_all | solution.py:255
  497.7 10.4 copy-start.16
  501.5 35.5 %all-to-all-start.7 = ((bf16[4,512,192]{1,2,0:T(8,128)(2,1)}), bf16[4,512,192]{1,2,0:T(8,128)(2,1)S(1)}, u32[]{:S(2)}, u32[]{:S(2)}) async-start(bf16[4,512,192]{1,2,0:T(8,128)(2,1)} %copy.111), calls=%async_computation.8 | async-start | bytes 1572864 | tf_op jit(solution)/shard_map/all_to_all | solution.py:255
  505.0 53.6 %reduce-scatter.5.cloned.1.call-start = ((), (), s32[]{:S(2)}) async-start(), calls=%async_computation.11 | async-start | bytes 1310720 | tf_op jit(solution)/shard_map/reduce_scatter | solution.py:258
  507.6 1016.5 %all-reduce.6.cloned.1.call-start = ((), (), s32[]{:S(2)}) async-start(), calls=%async_computation.13 | async-start | bytes 48041984
  512.5 24.5 %copy-start.101 = (f32[512]{0:T(512)S(1)}, f32[512]{0:T(512)}, u32[]{:S(2)}) copy-start(f32[512]{0:T(512)} %copy-done.99) | copy-start | bytes 6148
  537.0 10.1 copy-start.20
  547.9 12.4 copy-start.117
  551.0 15.5 copy-start.12
  593.1 10.0 copy-start.69
  593.1 12.1 copy-start.134
  593.1 15.7 copy-start.133
  625.4 49.6 %copy-start.106 = (f32[4,768]{1,0:T(4,128)S(1)}, f32[4,768]{1,0:T(4,128)}, u32[]{:S(2)}) copy-start(f32[4,768]{1,0:T(4,128)} %add.498) | copy-start | bytes 36868
  727.1 1031.3 %all-gather.4.cloned.1.call-start = ((), (), s32[]{:S(2)}) async-start(), calls=%async_computation.12 | async-start | bytes 54047232 | tf_op jit(solution)/shard_map/all_gather | solution.py:360
  (114 other events, 561.6 us)
Sparse Core Ops, SparseCore 0:
  432.4 37.6 reduce-scatter.2
  508.2 33.9 reduce-scatter.4
  727.2 796.9 all-reduce.5
  1536.8 221.6 all-gather.3
